TPU v7x, 256 devices: a whole 4x4x8 slice. The times are simulated.
256 devices in a mesh: layer: 4 (over y_lo, core), phi: 64 (over y_hi, z, x).
Axes of the slice: x: 4, y: 4 (y_hi: 2, y_lo: 2; y = y_hi * 2 + y_lo), z: 8, core: 2. Of those that a mesh axis runs over, the one named last changes fastest.
Arguments:
- hit_features: bfloat16 [4, 64, 1024, 128], P('layer', 'phi'), may hold values from -6 to 6
- edge_features: bfloat16 [4, 64, 4, 1024, 128], P('layer', 'phi'), may hold values from -6 to 6
- sender_slot: int32 [4, 64, 4, 1024], P('layer', 'phi'), may hold values from 0 to 1023
- receiver_slot: int32 [4, 64, 4, 1024], P('layer', 'phi'), may hold values from 0 to 1023
- edge_count: int32 [4, 64, 4], P('layer', 'phi'), may hold values from 0 to 1024, as said below
- grad_hits: bfloat16 [4, 64, 1024, 128], P('layer', 'phi'), may hold values from -6 to 6
- grad_edges: bfloat16 [4, 64, 4, 1024, 128], P('layer', 'phi'), may hold values from -6 to 6
- w_edge_in: bfloat16 [384, 128], replicated, may hold values from -0.3125 to 0.3125
- w_edge_out: bfloat16 [128, 128], replicated, may hold values from -0.5 to 0.5
- w_node_in: bfloat16 [256, 128], replicated, may hold values from -0.375 to 0.375
- w_node_out: bfloat16 [128, 128], replicated, may hold values from -0.5 to 0.5
Outputs:
- hit_grads: float32 [4, 64, 1024, 128], P('layer', 'phi')
- edge_grads: bfloat16 [4, 64, 4, 1024, 128], P('layer', 'phi')
- edge_in_grad: float32 [384, 128], replicated
- edge_out_grad: float32 [128, 128], replicated
- node_in_grad: float32 [256, 128], replicated
- node_out_grad: float32 [128, 128], replicated
Inputs may be any that keep to these rules, and one draw needn't show every extreme that they name: `edge_count`: live slots come first in each block. Kind 0 edges have their sender in the same shard, kind 1 in the previous layer group, kind 2 in the previous phi sector, kind 3 in the next one (phi closes into a loop). Kind 1 has no live slots in layer group 0. Some block is full in every draw. `sender_slot`: rows of dead slots are arbitrary. `receiver_slot`: rows of dead slots are arbitrary.
All inputs are finite; a program needn't handle non-finite values.
Results may differ from a plain program's by a relative error of at most 0.009.
Values may be sent and summed in bfloat16 or wider, within the bound.
A program may use at most 64 MiB of HBM per device.

v0:
```python
import jax
import jax.numpy as jnp
from jax import lax
from jax.sharding import PartitionSpec as P

norm_eps = 1e-05


def passed_along(value, axis, steps):
    count = lax.axis_size(axis)
    initial, last = (max(0, -steps), min(count, count - steps))
    return lax.ppermute(value, axis, [(source, source + steps) for source in range(initial, last)])


def passed_along_2(block, axis, distance):
    devices = range(lax.axis_size(axis))
    route = [((i - distance) % len(devices), i) for i in devices]
    return lax.ppermute(block, axis, route)


def norm_act(pre_act):
    average = jnp.mean(pre_act, axis=-1, keepdims=True)
    centred = pre_act - average
    spread = jnp.mean(centred * centred, axis=-1, keepdims=True)
    scaled = centred * lax.rsqrt(spread + norm_eps)
    return scaled * jax.nn.sigmoid(scaled)


def norm_act_back(pre_act, upstream):
    _, pullback = jax.vjp(norm_act, pre_act)
    return pullback(upstream)[0]


def one_hot_rows(indices, node_total):
    return (indices[:, None] == lax.iota(jnp.int32, node_total)[None, :]).astype(jnp.bfloat16)


def pick_rows(selector, table):
    return jnp.dot(selector, table, preferred_element_type=jnp.float32)


def split_parts(values):
    upper = values.astype(jnp.bfloat16)
    lower = (values - upper.astype(jnp.float32)).astype(jnp.bfloat16)
    return (upper, lower)


def add_rows(selector, values):
    upper, lower = split_parts(values)
    dims = (((0,), (0,)), ((), ()))
    first = lax.dot_general(selector, upper, dims, preferred_element_type=jnp.float32)
    second = lax.dot_general(selector, lower, dims, preferred_element_type=jnp.float32)
    return first + second


def body(
    hit_features,
    edge_features,
    sender_slot,
    receiver_slot,
    edge_count,
    grad_hits,
    grad_edges,
    w_edge_in,
    w_edge_out,
    w_node_in,
    w_node_out,
):
    local_rows = hit_features[0, 0]
    node_total = local_rows.shape[0]
    features = local_rows.shape[1]
    send_all = sender_slot[0, 0]
    recv_all = receiver_slot[0, 0]
    counts = edge_count[0, 0]
    edge_all = edge_features[0, 0]
    grad_edge_all = grad_edges[0, 0]
    grad_local = grad_hits[0, 0]
    kind_total = send_all.shape[0]
    capacity = send_all.shape[1]
    tile_rows = 256
    tile_total = capacity // tile_rows
    lower_rows = passed_along(local_rows, "layer", 1)
    prev_rows = passed_along_2(local_rows, "phi", 1)
    next_rows = passed_along_2(local_rows, "phi", -1)
    sources = (local_rows, lower_rows, prev_rows, next_rows)
    positions = lax.iota(jnp.int32, capacity)
    live_all = (positions[None, :] < counts[:, None]).astype(jnp.float32)

    def tile_indices(k, offset):
        send_idx = lax.dynamic_slice_in_dim(send_all[k], offset, tile_rows, 0)
        recv_idx = lax.dynamic_slice_in_dim(recv_all[k], offset, tile_rows, 0)
        live_mask = lax.dynamic_slice_in_dim(live_all[k], offset, tile_rows, 0)
        return (send_idx, recv_idx, live_mask)

    def forward_tile(k, offset, send_hot, recv_hot):
        edge_rows = lax.dynamic_slice_in_dim(edge_all[k], offset, tile_rows, 0)
        sender_rows = pick_rows(send_hot, sources[k]).astype(jnp.bfloat16)
        receiver_rows = pick_rows(recv_hot, local_rows).astype(jnp.bfloat16)
        inputs = jnp.concatenate([sender_rows, receiver_rows, edge_rows], axis=-1)
        pre_act = jnp.dot(inputs, w_edge_in, preferred_element_type=jnp.float32)
        hidden = norm_act(pre_act).astype(jnp.bfloat16)
        return (inputs, pre_act, hidden)

    def run_tiles(tile_step, totals):

        def looped(number, inner):
            return tile_step(number * tile_rows, inner)

        return lax.fori_loop(0, tile_total, looped, totals)

    incoming = jnp.zeros((node_total, features), jnp.float32)
    stored = []
    for k in range(kind_total):

        def message_step(offset, totals):
            total, kept = totals
            send_idx, recv_idx, live_mask = tile_indices(k, offset)
            send_hot = one_hot_rows(send_idx, node_total)
            recv_hot = one_hot_rows(recv_idx, node_total)
            inputs, pre_act, hidden = forward_tile(k, offset, send_hot, recv_hot)
            message = (
                jnp.dot(hidden, w_edge_out, preferred_element_type=jnp.float32) * live_mask[:, None]
            )
            total = total + add_rows(recv_hot, message)
            kept = (
                lax.dynamic_update_slice_in_dim(kept[0], inputs, offset, 0),
                lax.dynamic_update_slice_in_dim(kept[1], pre_act, offset, 0),
                lax.dynamic_update_slice_in_dim(kept[2], hidden, offset, 0),
            )
            return (total, kept)

        kept_start = (
            jnp.zeros((capacity, 3 * features), jnp.bfloat16),
            jnp.zeros((capacity, features), jnp.float32),
            jnp.zeros((capacity, features), jnp.bfloat16),
        )
        incoming, kept_done = run_tiles(message_step, (incoming, kept_start))
        stored.append(kept_done)
    incoming = incoming.astype(jnp.bfloat16)
    node_in = jnp.concatenate([local_rows, incoming], axis=-1)
    node_pre = jnp.dot(node_in, w_node_in, preferred_element_type=jnp.float32)
    node_hidden = norm_act(node_pre).astype(jnp.bfloat16)
    node_hidden_grad = jnp.dot(grad_local, w_node_out.T, preferred_element_type=jnp.float32)
    node_out_part = jnp.dot(node_hidden.T, grad_local, preferred_element_type=jnp.float32)
    node_pre_grad = norm_act_back(node_pre, node_hidden_grad).astype(jnp.bfloat16)
    node_input_grad = jnp.dot(node_pre_grad, w_node_in.T, preferred_element_type=jnp.float32)
    node_in_part = jnp.dot(node_in.T, node_pre_grad, preferred_element_type=jnp.float32)
    incoming_upper, incoming_lower = split_parts(node_input_grad[:, features:])
    recv_total = jnp.zeros((node_total, features), jnp.float32)
    in_total = jnp.zeros((3 * features, features), jnp.float32)
    out_total = jnp.zeros((features, features), jnp.float32)
    send_parts = []
    edge_parts = []
    for k in range(kind_total):

        def back_step(offset, totals):
            recv_sum, send_sum, in_sum, out_sum, edge_done = totals
            send_idx, recv_idx, live_mask = tile_indices(k, offset)
            send_hot = one_hot_rows(send_idx, node_total)
            recv_hot = one_hot_rows(recv_idx, node_total)
            inputs = lax.dynamic_slice_in_dim(stored[k][0], offset, tile_rows, 0)
            pre_act = lax.dynamic_slice_in_dim(stored[k][1], offset, tile_rows, 0)
            hidden = lax.dynamic_slice_in_dim(stored[k][2], offset, tile_rows, 0)
            grad_rows = lax.dynamic_slice_in_dim(grad_edge_all[k], offset, tile_rows, 0)
            picked = pick_rows(recv_hot, incoming_upper) + pick_rows(recv_hot, incoming_lower)
            message_grad = (live_mask[:, None] * (grad_rows.astype(jnp.float32) + picked)).astype(
                jnp.bfloat16
            )
            hidden_grad = jnp.dot(message_grad, w_edge_out.T, preferred_element_type=jnp.float32)
            pre_grad = norm_act_back(pre_act, hidden_grad).astype(jnp.bfloat16)
            input_grad = jnp.dot(pre_grad, w_edge_in.T, preferred_element_type=jnp.float32)
            edge_new = (grad_rows.astype(jnp.float32) + input_grad[:, 2 * features :]).astype(
                jnp.bfloat16
            )
            edge_done = lax.dynamic_update_slice_in_dim(edge_done, edge_new, offset, 0)
            recv_sum = recv_sum + add_rows(recv_hot, input_grad[:, features : 2 * features])
            send_sum = send_sum + add_rows(send_hot, input_grad[:, :features])
            in_sum = in_sum + jnp.dot(inputs.T, pre_grad, preferred_element_type=jnp.float32)
            out_sum = out_sum + jnp.dot(hidden.T, message_grad, preferred_element_type=jnp.float32)
            return (recv_sum, send_sum, in_sum, out_sum, edge_done)

        start_totals = (
            recv_total,
            jnp.zeros((node_total, features), jnp.float32),
            in_total,
            out_total,
            grad_edge_all[k],
        )
        recv_total, send_sum, in_total, out_total, edge_done = run_tiles(back_step, start_totals)
        send_parts.append(send_sum)
        edge_parts.append(edge_done)
    from_upper = passed_along(send_parts[1].astype(jnp.bfloat16), "layer", -1).astype(jnp.float32)
    from_next = passed_along_2(send_parts[2].astype(jnp.bfloat16), "phi", -1).astype(jnp.float32)
    from_prev = passed_along_2(send_parts[3].astype(jnp.bfloat16), "phi", 1).astype(jnp.float32)
    returned = from_next + from_prev
    hit_total = (
        grad_local.astype(jnp.float32)
        + node_input_grad[:, :features]
        + recv_total
        + send_parts[0]
        + from_upper
        + returned
    )
    summed = lax.psum((in_total, out_total, node_in_part, node_out_part), ("layer", "phi"))
    shard_count = lax.axis_size("layer") * lax.axis_size("phi")
    edge_stack = jnp.stack(edge_parts)
    return (
        hit_total[None, None],
        edge_stack[None, None],
        summed[0] / shard_count,
        summed[1] / shard_count,
        summed[2] / shard_count,
        summed[3] / shard_count,
    )


def solution(mesh):
    placed = (
        P("layer", "phi", None, None),
        P("layer", "phi", None, None, None),
        P("layer", "phi", None, None),
        P("layer", "phi", None, None),
        P("layer", "phi", None),
        P("layer", "phi", None, None),
        P("layer", "phi", None, None, None),
        P(),
        P(),
        P(),
        P(),
    )
    return jax.shard_map(
        body,
        mesh=mesh,
        in_specs=placed,
        out_specs=(
            P("layer", "phi", None, None),
            P("layer", "phi", None, None, None),
            P(),
            P(),
            P(),
            P(),
        ),
        check_vma=False,
    )
```

profile of v0, /device:TPU:2, one launch (start us, length us, event | category | flops | bytes accessed | tf_op | source)
XLA Modules:
  0.0 593.0 jit_solution(756839716940063795)
XLA Ops:
  7.2 2.4 collective-permute-start
  16.6 33.2 %while.168 = (s32[]{:T(128)}, f32[1024,128]{1,0:T(8,128)S(1)}, bf16[1024,384]{0,1:T(8,128)(2,1)}, f32[1024,128]{0,1:T(8,128)}, bf16[1024,128]{0,1:T(8,128)(2,1)S...) while((s32[]{:T(128)}, f32[1024,128]{1,0:T(8,128)S(1)}, ...), condition=%wide.region_3.0_spmd.clone, body=%wide.region_0.0_spmd.clone.sunk | while | flops 305463552 | bytes 8575457 | solution.py:109
  54.2 26.9 %while.165 = (s32[]{:T(128)}, f32[1024,128]{1,0:T(8,128)S(1)}, bf16[1024,384]{0,1:T(8,128)(2,1)}, f32[1024,128]{0,1:T(8,128)}, bf16[1024,128]{0,1:T(8,128)(2,1)}...) while((s32[]{:T(128)}, f32[1024,128]{1,0:T(8,128)S(1)}, ...), condition=%wide.region_7.0_spmd, body=%wide.region_4.0_spmd.sunk | while | flops 305332480 | bytes 5421311 | solution.py:109
  83.7 27.0 %while.166 = (s32[]{:T(128)}, f32[1024,128]{1,0:T(8,128)S(1)}, bf16[1024,384]{0,1:T(8,128)(2,1)}, f32[1024,128]{0,1:T(8,128)}, bf16[1024,128]{0,1:T(8,128)(2,1)}...) while((s32[]{:T(128)}, f32[1024,128]{1,0:T(8,128)S(1)}, ...), condition=%wide.region_11.0_spmd, body=%wide.region_8.0_spmd.sunk | while | flops 305332480 | bytes 5421311 | solution.py:109
  113.3 27.0 %while.167 = (s32[]{:T(128)}, f32[1024,128]{1,0:T(8,128)S(1)}, bf16[1024,384]{0,1:T(8,128)(2,1)}, f32[1024,128]{0,1:T(8,128)}, bf16[1024,128]{0,1:T(8,128)(2,1)}...) while((s32[]{:T(128)}, f32[1024,128]{1,0:T(8,128)S(1)}, ...), condition=%wide.region_15.0_spmd, body=%wide.region_12.0_spmd.sunk | while | flops 305332480 | bytes 5421311 | solution.py:109
  144.1 1.9 fusion.147
  148.2 51.9 %while.169 = (s32[]{:T(128)}, f32[1024,128]{1,0:T(8,128)S(1)}, f32[1024,128]{1,0:T(8,128)}, f32[384,128]{1,0:T(8,128)S(1)}, f32[128,128]{1,0:T(8,128)S(1)}, /*in...) while((s32[]{:T(128)}, f32[1024,128]{1,0:T(8,128)S(1)}, ...), condition=%wide.region_25.26_spmd.clone, body=%wide.region_20.25_spmd.clone.sunk | while | flops 473990912 | bytes 11069784 | solution.py:109
  167.1 2.4 fusion.376
  180.4 2.4 fusion.376
  193.6 2.4 fusion.376
  200.1 40.0 %while.170 = (s32[]{:T(128)}, f32[1024,128]{1,0:T(8,128)S(1)}, f32[1024,128]{1,0:T(8,128)}, f32[384,128]{1,0:T(8,128)S(1)}, f32[128,128]{1,0:T(8,128)S(1)}, /*in...) while((s32[]{:T(128)}, f32[1024,128]{1,0:T(8,128)S(1)}, ...), condition=%wide.region_31.0_spmd.clone, body=%wide.region_26.31_spmd.clone.sunk | while | flops 473794304 | bytes 13166961 | solution.py:109
  213.1 2.4 fusion.394
  223.4 2.4 fusion.394
  233.6 2.4 fusion.394
  240.1 39.9 %while.171 = (s32[]{:T(128)}, f32[1024,128]{1,0:T(8,128)S(1)}, f32[1024,128]{1,0:T(8,128)}, f32[384,128]{1,0:T(8,128)S(1)}, f32[128,128]{1,0:T(8,128)S(1)}, /*in...) while((s32[]{:T(128)}, f32[1024,128]{1,0:T(8,128)S(1)}, ...), condition=%wide.region_37.38_spmd.clone, body=%wide.region_32.37_spmd.clone.sunk | while | flops 473794304 | bytes 13166961 | solution.py:109
  253.1 2.4 fusion.412
  263.3 2.4 fusion.412
  273.6 2.4 fusion.412
  280.1 39.9 %while.172 = (s32[]{:T(128)}, f32[1024,128]{1,0:T(8,128)S(1)}, f32[1024,128]{1,0:T(8,128)}, f32[384,128]{1,0:T(8,128)S(1)}, f32[128,128]{1,0:T(8,128)S(1)}, /*in...) while((s32[]{:T(128)}, f32[1024,128]{1,0:T(8,128)S(1)}, ...), condition=%wide.region_43.44_spmd.clone, body=%wide.region_38.43_spmd.clone.sunk | while | flops 473794304 | bytes 13166961 | solution.py:109
  293.0 2.4 fusion.430
  303.2 2.4 fusion.430
  313.5 2.4 fusion.430
  324.7 7.7 %collective-permute-start.4 = (bf16[1024,128]{1,0:T(8,128)(2,1)}, bf16[1024,128]{1,0:T(8,128)(2,1)S(1)}, u32[]{:S(2)}, u32[]{:S(2)}) collective-permute-start(bf16[1024,128]{1,0:T(8,128)(2,1)} %convert_element_type.563), channel_id=1, source_target_pairs={{1,0},{2,1},{3,2},{4,3},{5,4},{6,5},{7,6},{8,7},{9,8},{10,9},{11,1... | collective-permute-start | bytes 786440 | tf_op jit(solution)/shard_map/ppermute | solution.py:18
  335.6 244.9 %all-reduce.3.cloned.1.call-done = (f32[384,128]{1,0:T(8,128)}, f32[128,128]{1,0:T(8,128)}, f32[256,128]{1,0:T(8,128)}, f32[128,128]{1,0:T(8,128)}) async-done(((f32[384,128]{1,0:T(8,128)}, f32[128,128]{1,0:T(8,128)}, f32[256,128]{1,0:T(8,128)}, f32[128,128]{1,0:T(8,128)}), (f32[384,128]{1,0:T(8,128)}, f32[128,128]{1,0:T(8,128)}, f32[256,128]{1,0:T(8,128)}, ...) | async-done | bytes 458768 | tf_op jit(solution)/shard_map/psum | solution.py:204
  (946 shorter events, 288.8 us)
Async XLA Ops:
  7.2 133.1 %copy-start = (bf16[256,128]{1,0:T(8,128)(2,1)S(1)}, bf16[256,128]{1,0:T(8,128)(2,1)}, u32[]{:S(2)}) copy-start(bf16[256,128]{1,0:T(8,128)(2,1)} %param.36) | copy-start | bytes 196612
  7.2 573.2 %all-reduce.3.cloned.1.call-start = ((), (), s32[]{:S(2)}) async-start(), calls=%async_computation | async-start | bytes 917504 | tf_op jit(solution)/shard_map/psum | solution.py:204
  7.2 44.3 %collective-permute-start = (bf16[1024,128]{1,0:T(8,128)(2,1)}, bf16[1024,128]{1,0:T(8,128)(2,1)}, u32[]{:S(2)}, u32[]{:S(2)}) collective-permute-start(bf16[1024,128]{1,0:T(8,128)(2,1)} %bitcast.13), channel_id=1, source_target_pairs={{0,64},{64,128},{128,192},{1,65},{65,129},{129,193},{2,66},{66,130... | collective-permute-start | bytes 786440 | tf_op jit(solution)/shard_map/ppermute | solution.py:12
  9.7 71.4 %collective-permute-start.1 = (bf16[1024,128]{1,0:T(8,128)(2,1)}, bf16[1024,128]{1,0:T(8,128)(2,1)}, u32[]{:S(2)}, u32[]{:S(2)}) collective-permute-start(bf16[1024,128]{1,0:T(8,128)(2,1)} %bitcast.13), channel_id=1, source_target_pairs={{63,0},{0,1},{1,2},{2,3},{3,4},{4,5},{5,6},{6,7},{7,8},{8,9},{9,10... | collective-permute-start | bytes 786440 | tf_op jit(solution)/shard_map/ppermute | solution.py:18
  11.2 99.5 %collective-permute-start.2 = (bf16[1024,128]{1,0:T(8,128)(2,1)}, bf16[1024,128]{1,0:T(8,128)(2,1)}, u32[]{:S(2)}, u32[]{:S(2)}) collective-permute-start(bf16[1024,128]{1,0:T(8,128)(2,1)} %bitcast.13), channel_id=1, source_target_pairs={{1,0},{2,1},{3,2},{4,3},{5,4},{6,5},{7,6},{8,7},{9,8},{10,9},{11,1... | collective-permute-start | bytes 786440 | tf_op jit(solution)/shard_map/ppermute | solution.py:18
  16.6 33.9 %copy-start.3 = (bf16[1,1,4,1024,128]{4,3,2,1,0:T(8,128)(2,1)S(1)}, bf16[1,1,4,1024,128]{4,3,2,1,0:T(8,128)(2,1)}, u32[]{:S(2)}) copy-start(bf16[1,1,4,1024,128]{4,3,2,1,0:T(8,128)(2,1)} %param.33) | copy-start | bytes 3145732
  16.7 5.4 copy-start.37
  25.0 5.4 copy-start.37
  33.3 5.4 copy-start.37
  41.6 5.4 copy-start.37
  219.6 1.5 copy-start.31
  240.1 1.5 copy-start.33
  320.0 3.9 copy-start.6
  322.4 9.9 %copy-start.7 = (f32[1024,128]{1,0:T(8,128)S(1)}, f32[1024,128]{1,0:T(8,128)}, u32[]{:S(2)}) copy-start(f32[1024,128]{1,0:T(8,128)} %get-tuple-element.1998) | copy-start | bytes 1572868
  322.4 262.7 %collective-permute-start.5 = (bf16[1024,128]{1,0:T(8,128)(2,1)}, bf16[1024,128]{1,0:T(8,128)(2,1)S(1)}, u32[]{:S(2)}, u32[]{:S(2)}) collective-permute-start(bf16[1024,128]{1,0:T(8,128)(2,1)} %convert_element_type.565), channel_id=1, source_target_pairs={{63,0},{0,1},{1,2},{2,3},{3,4},{4,5},{5,6},{6,7},{7,8},{8,9},{9,10... | collective-permute-start | bytes 786440 | tf_op jit(solution)/shard_map/ppermute | solution.py:18
  323.9 10.5 %copy-start.26 = (bf16[1024,128]{1,0:T(8,128)(2,1)S(1)}, bf16[1024,128]{1,0:T(8,128)(2,1)}, u32[]{:S(2)}) copy-start(bf16[1024,128]{1,0:T(8,128)(2,1)} %get-tuple-element.2001) | copy-start | bytes 786436
  324.7 260.5 %collective-permute-start.4 = (bf16[1024,128]{1,0:T(8,128)(2,1)}, bf16[1024,128]{1,0:T(8,128)(2,1)S(1)}, u32[]{:S(2)}, u32[]{:S(2)}) collective-permute-start(bf16[1024,128]{1,0:T(8,128)(2,1)} %convert_element_type.563), channel_id=1, source_target_pairs={{1,0},{2,1},{3,2},{4,3},{5,4},{6,5},{7,6},{8,7},{9,8},{10,9},{11,1... | collective-permute-start | bytes 786440 | tf_op jit(solution)/shard_map/ppermute | solution.py:18
  332.4 2.0 copy-start.23
  332.4 2.0 copy-start.24
  332.4 2.1 copy-start.25
  333.1 252.1 %collective-permute-start.3 = (bf16[1024,128]{1,0:T(8,128)(2,1)}, bf16[1024,128]{1,0:T(8,128)(2,1)S(1)}, u32[]{:S(2)}, u32[]{:S(2)}) collective-permute-start(bf16[1024,128]{1,0:T(8,128)(2,1)} %convert_element_type.561), channel_id=1, source_target_pairs={{64,0},{128,64},{192,128},{65,1},{129,65},{193,129},{66,2},{130,66... | collective-permute-start | bytes 786440 | tf_op jit(solution)/shard_map/ppermute | solution.py:12
  334.4 250.7 %copy-start.13 = (f32[1024,256]{1,0:T(8,128)S(1)}, f32[1024,256]{1,0:T(8,128)}, u32[]{:S(2)}) copy-start(f32[1024,256]{1,0:T(8,128)} %copy-done.12) | copy-start | bytes 3145732
  335.6 249.6 %copy-start.8 = (f32[1024,128]{1,0:T(8,128)S(1)}, f32[1024,128]{1,0:T(8,128)}, u32[]{:S(2)}) copy-start(f32[1024,128]{1,0:T(8,128)} %get-tuple-element.1997) | copy-start | bytes 1572868
  583.5 1.7 copy-start.28
  (98 other events, 96.8 us)
Sparse Core Ops, SparseCore 0:
  320.8 259.5 all-reduce.2
where the time goes:
time: 598 us; the launch traced here: 593 us
  waiting for transfers between devices  245 us (41%)
  matrix products  212 us (35%)
  other arithmetic  66.8 us (11%)
  local copies, waits for them, and re-layouts  36.3 us (6%)
  starting transfers between devices  15 us (3%)
  between operations  14.3 us (2%)
    psum x1, waiting for transfers between devices, body(): lax.psum((in_total, out_total, node_in_part, node_out_part), ('layer', 'p...  245 us
    dot_general x64, matrix products, pick_rows(): return jnp.dot(selector, table, preferred_element_type=jnp.float32)  71.2 us
    dot_general x48, matrix products, add_rows(): lax.dot_general(selector, lower, dims, preferred_element_type=jnp.float32)  55.7 us
    dot_general x48, matrix products, add_rows(): lax.dot_general(selector, upper, dims, preferred_element_type=jnp.float32)  26.7 us
    dot_general x16, matrix products, back_step(): jnp.dot(inputs.T, pre_grad, preferred_element_type=jnp.float32)  18.4 us
    while x184, local copies, waits for them, and re-layouts  17.3 us
    dot_general x16, matrix products, back_step(): jnp.dot(hidden.T, message_grad, preferred_element_type=jnp.float32)  16.4 us
  transfers between devices with their start and end apart: 7, of which 1 were waited for; matrix products, arithmetic and copies ran while one was open for 16% of the time, Pallas kernels for 0%

commit v1 on v0

--- a/solution.py
+++ b/solution.py
@@ -201,7 +201,7 @@
         + from_upper
         + returned
     )
-    summed = lax.psum((in_total, out_total, node_in_part, node_out_part), ("layer", "phi"))
+    summed = lax.psum(lax.psum((in_total, out_total, node_in_part, node_out_part), "phi"), "layer")
     shard_count = lax.axis_size("layer") * lax.axis_size("phi")
     edge_stack = jnp.stack(edge_parts)
     return (

time: 598 us -> 1080 us (1.81)
  waiting for transfers between devices: 245 us -> 715 us
  local copies, waits for them, and re-layouts: 36.3 us -> 66.5 us
  matrix products: 212 us -> 190 us
    psum x1 -> x2, waiting for transfers between devices: 245 us -> 715 us  [the longest x1 673 us: body(): lax.psum((in_total, out_total, node_in_part, node_out_part), 'phi')]
    while x184 -> x376, local copies, waits for them, and re-layouts: 17.3 us -> 47.2 us
    dot_general x64, matrix products: 71.2 us -> 47.4 us  [pick_rows(): return jnp.dot(selector, table, preferred_element_type=jnp.float32)]
  transfers between devices with their start and end apart: 7 -> 8, of which waited for: 1 -> 2; matrix products, arithmetic and copies ran while one was open for 16% -> 9% of each run, Pallas kernels for 0% -> 0%
where the time goes in v1:
time: 1080 us; the launch traced here: 1070 us
  waiting for transfers between devices  715 us (66%)
  matrix products  190 us (18%)
  other arithmetic  69 us (6%)
  local copies, waits for them, and re-layouts  66.5 us (6%)
  starting transfers between devices  15.2 us (1%)
  between operations  14.3 us (1%)
    psum x1, waiting for transfers between devices, body(): lax.psum((in_total, out_total, node_in_part, node_out_part), 'phi')  673 us
    dot_general x48, matrix products, add_rows(): lax.dot_general(selector, lower, dims, preferred_element_type=jnp.float32)  59.6 us
    dot_general x64, matrix products, pick_rows(): return jnp.dot(selector, table, preferred_element_type=jnp.float32)  47.4 us
    while x376, local copies, waits for them, and re-layouts  47.2 us
    psum x1, waiting for transfers between devices, body(): lax.psum(lax.psum((in_total, out_total, node_in_part, node_out_part), 'ph...  41.9 us
    dot_general x48, matrix products, add_rows(): lax.dot_general(selector, upper, dims, preferred_element_type=jnp.float32)  26.7 us
  transfers between devices with their start and end apart: 8, of which 2 were waited for; matrix products, arithmetic and copies ran while one was open for 9% of the time, Pallas kernels for 0%

profile of v1, /device:TPU:2, one launch (start us, length us, event | category | flops | bytes accessed | tf_op | source)
XLA Modules:
  0.0 1074.6 jit_solution(5720589740726439456)
XLA Ops:
  7.2 2.5 collective-permute-start
  16.7 31.7 %while.168 = (s32[]{:T(128)}, f32[1024,128]{1,0:T(8,128)S(1)}, bf16[1024,384]{0,1:T(8,128)(2,1)}, f32[1024,128]{0,1:T(8,128)}, bf16[1024,128]{0,1:T(8,128)(2,1)}...) while((s32[]{:T(128)}, f32[1024,128]{1,0:T(8,128)S(1)}, ...), condition=%wide.region_3.0_spmd.clone, body=%wide.region_0.0_spmd.clone.sunk | while | flops 305463552 | bytes 8051185 | solution.py:109
  52.1 27.0 %while.165 = (s32[]{:T(128)}, f32[1024,128]{1,0:T(8,128)S(1)}, bf16[1024,384]{0,1:T(8,128)(2,1)}, f32[1024,128]{0,1:T(8,128)}, bf16[1024,128]{0,1:T(8,128)(2,1)}...) while((s32[]{:T(128)}, f32[1024,128]{1,0:T(8,128)S(1)}, ...), condition=%wide.region_7.0_spmd, body=%wide.region_4.0_spmd.sunk | while | flops 305332480 | bytes 5421311 | solution.py:109
  81.7 27.0 %while.166 = (s32[]{:T(128)}, f32[1024,128]{1,0:T(8,128)S(1)}, bf16[1024,384]{0,1:T(8,128)(2,1)}, f32[1024,128]{0,1:T(8,128)}, bf16[1024,128]{0,1:T(8,128)(2,1)}...) while((s32[]{:T(128)}, f32[1024,128]{1,0:T(8,128)S(1)}, ...), condition=%wide.region_11.0_spmd, body=%wide.region_8.0_spmd.sunk | while | flops 305332480 | bytes 5421311 | solution.py:109
  111.3 27.0 %while.167 = (s32[]{:T(128)}, f32[1024,128]{1,0:T(8,128)S(1)}, bf16[1024,384]{0,1:T(8,128)(2,1)}, f32[1024,128]{0,1:T(8,128)}, bf16[1024,128]{0,1:T(8,128)(2,1)}...) while((s32[]{:T(128)}, f32[1024,128]{1,0:T(8,128)S(1)}, ...), condition=%wide.region_15.0_spmd, body=%wide.region_12.0_spmd.sunk | while | flops 305332480 | bytes 5421311 | solution.py:109
  144.5 55.4 %while.169 = (s32[]{:T(128)}, f32[1024,128]{1,0:T(8,128)S(1)}, f32[1024,128]{1,0:T(8,128)}, f32[384,128]{1,0:T(8,128)S(1)}, f32[128,128]{1,0:T(8,128)S(1)}, /*in...) while((s32[]{:T(128)}, f32[1024,128]{1,0:T(8,128)S(1)}, ...), condition=%wide.region_25.26_spmd.clone, body=%wide.region_20.25_spmd.clone.sunk | while | flops 473990912 | bytes 12265984 | solution.py:109
  165.1 2.4 fusion.376
  179.2 2.4 fusion.376
  193.3 2.4 fusion.376
  199.9 43.7 %while.170 = (s32[]{:T(128)}, f32[1024,128]{1,0:T(8,128)S(1)}, f32[1024,128]{1,0:T(8,128)}, f32[384,128]{1,0:T(8,128)S(1)}, f32[128,128]{1,0:T(8,128)S(1)}, /*in...) while((s32[]{:T(128)}, f32[1024,128]{1,0:T(8,128)S(1)}, ...), condition=%wide.region_31.0_spmd.clone, body=%wide.region_26.31_spmd.clone.sunk | while | flops 473794304 | bytes 14363161 | solution.py:109
  214.7 2.4 fusion.394
  225.9 2.4 fusion.394
  237.1 2.4 fusion.394
  243.6 43.7 %while.171 = (s32[]{:T(128)}, f32[1024,128]{1,0:T(8,128)S(1)}, f32[1024,128]{1,0:T(8,128)}, f32[384,128]{1,0:T(8,128)S(1)}, f32[128,128]{1,0:T(8,128)S(1)}, /*in...) while((s32[]{:T(128)}, f32[1024,128]{1,0:T(8,128)S(1)}, ...), condition=%wide.region_37.38_spmd.clone, body=%wide.region_32.37_spmd.clone.sunk | while | flops 473794304 | bytes 14363161 | solution.py:109
  258.4 2.4 fusion.412
  269.6 2.4 fusion.412
  280.8 2.4 fusion.412
  287.3 43.7 %while.172 = (s32[]{:T(128)}, f32[1024,128]{1,0:T(8,128)S(1)}, f32[1024,128]{1,0:T(8,128)}, f32[384,128]{1,0:T(8,128)S(1)}, f32[128,128]{1,0:T(8,128)S(1)}, /*in...) while((s32[]{:T(128)}, f32[1024,128]{1,0:T(8,128)S(1)}, ...), condition=%wide.region_43.44_spmd.clone, body=%wide.region_38.43_spmd.clone.sunk | while | flops 473794304 | bytes 14363161 | solution.py:109
  302.1 2.4 fusion.430
  313.2 2.4 fusion.430
  324.4 2.4 fusion.430
  335.7 7.7 collective-permute-start.4
  345.6 673.1 %all-reduce.5.cloned.1.call-done = (f32[384,128]{1,0:T(8,128)}, f32[128,128]{1,0:T(8,128)}, f32[256,128]{1,0:T(8,128)}, f32[128,128]{1,0:T(8,128)}) async-done(((f32[384,128]{1,0:T(8,128)}, f32[128,128]{1,0:T(8,128)}, f32[256,128]{1,0:T(8,128)}, f32[128,128]{1,0:T(8,128)}), (f32[384,128]{1,0:T(8,128)}, f32[128,128]{1,0:T(8,128)}, f32[256,128]{1,0:T(8,128)}, ...) | async-done | bytes 458768 | tf_op jit(solution)/shard_map/psum | solution.py:204
  1022.6 41.9 %all-reduce.7.cloned.1.call-done = (f32[384,128]{1,0:T(8,128)}, f32[128,128]{1,0:T(8,128)}, f32[256,128]{1,0:T(8,128)}, f32[128,128]{1,0:T(8,128)}) async-done(((f32[384,128]{1,0:T(8,128)}, f32[128,128]{1,0:T(8,128)}, f32[256,128]{1,0:T(8,128)}, f32[128,128]{1,0:T(8,128)}), (f32[384,128]{1,0:T(8,128)}, f32[128,128]{1,0:T(8,128)}, f32[256,128]{1,0:T(8,128)}, ...) | async-done | bytes 458768 | tf_op jit(solution)/shard_map/psum | solution.py:204
  (1149 shorter events, 301.4 us)
Async XLA Ops:
  7.2 131.1 %copy-start = (bf16[256,128]{1,0:T(8,128)(2,1)S(1)}, bf16[256,128]{1,0:T(8,128)(2,1)}, u32[]{:S(2)}) copy-start(bf16[256,128]{1,0:T(8,128)(2,1)} %param.36) | copy-start | bytes 196612
  7.2 1011.5 %all-reduce.5.cloned.1.call-start = ((), (), s32[]{:S(2)}) async-start(), calls=%async_computation | async-start | bytes 917504 | tf_op jit(solution)/shard_map/psum | solution.py:204
  7.2 42.2 %collective-permute-start = (bf16[1024,128]{1,0:T(8,128)(2,1)}, bf16[1024,128]{1,0:T(8,128)(2,1)}, u32[]{:S(2)}, u32[]{:S(2)}) collective-permute-start(bf16[1024,128]{1,0:T(8,128)(2,1)} %bitcast.285), channel_id=1, source_target_pairs={{0,64},{64,128},{128,192},{1,65},{65,129},{129,193},{2,66},{66,130... | collective-permute-start | bytes 786440 | tf_op jit(solution)/shard_map/ppermute | solution.py:12
  9.7 69.4 %collective-permute-start.1 = (bf16[1024,128]{1,0:T(8,128)(2,1)}, bf16[1024,128]{1,0:T(8,128)(2,1)}, u32[]{:S(2)}, u32[]{:S(2)}) collective-permute-start(bf16[1024,128]{1,0:T(8,128)(2,1)} %bitcast.286), channel_id=1, source_target_pairs={{63,0},{0,1},{1,2},{2,3},{3,4},{4,5},{5,6},{6,7},{7,8},{8,9},{9,10... | collective-permute-start | bytes 786440 | tf_op jit(solution)/shard_map/ppermute | solution.py:18
  11.2 97.6 %collective-permute-start.2 = (bf16[1024,128]{1,0:T(8,128)(2,1)}, bf16[1024,128]{1,0:T(8,128)(2,1)}, u32[]{:S(2)}, u32[]{:S(2)}) collective-permute-start(bf16[1024,128]{1,0:T(8,128)(2,1)} %bitcast.287), channel_id=1, source_target_pairs={{1,0},{2,1},{3,2},{4,3},{5,4},{6,5},{7,6},{8,7},{9,8},{10,9},{11,1... | collective-permute-start | bytes 786440 | tf_op jit(solution)/shard_map/ppermute | solution.py:18
  16.7 31.7 %copy-start.3 = (bf16[1,1,4,1024,128]{4,3,2,1,0:T(8,128)(2,1)S(1)}, bf16[1,1,4,1024,128]{4,3,2,1,0:T(8,128)(2,1)}, u32[]{:S(2)}) copy-start(bf16[1,1,4,1024,128]{4,3,2,1,0:T(8,128)(2,1)} %param.33) | copy-start | bytes 3145732
  16.7 3.4 copy-start.58
  24.7 3.4 copy-start.58
  32.6 3.3 copy-start.58
  40.5 3.4 copy-start.58
  144.5 6.3 copy-start.50
  157.6 6.3 copy-start.50
  171.7 6.3 copy-start.50
  185.8 6.3 copy-start.50
  330.9 4.0 copy-start.6
  331.6 732.9 %all-reduce.7.cloned.1.call-start = ((), (), s32[]{:S(2)}) async-start(), calls=%async_computation.1 | async-start | bytes 917504 | tf_op jit(solution)/shard_map/psum | solution.py:204
  333.5 9.9 copy-start.7
  333.5 686.4 %collective-permute-start.5 = (bf16[1024,128]{1,0:T(8,128)(2,1)}, bf16[1024,128]{1,0:T(8,128)(2,1)}, u32[]{:S(2)}, u32[]{:S(2)}) collective-permute-start(bf16[1024,128]{1,0:T(8,128)(2,1)} %convert_element_type.565), channel_id=1, source_target_pairs={{63,0},{0,1},{1,2},{2,3},{3,4},{4,5},{5,6},{6,7},{7,8},{8,9},{9,10... | collective-permute-start | bytes 786440 | tf_op jit(solution)/shard_map/ppermute | solution.py:18
  335.7 684.2 %collective-permute-start.4 = (bf16[1024,128]{1,0:T(8,128)(2,1)}, bf16[1024,128]{1,0:T(8,128)(2,1)}, u32[]{:S(2)}, u32[]{:S(2)}) collective-permute-start(bf16[1024,128]{1,0:T(8,128)(2,1)} %convert_element_type.563), channel_id=1, source_target_pairs={{1,0},{2,1},{3,2},{4,3},{5,4},{6,5},{7,6},{8,7},{9,8},{10,9},{11,1... | collective-permute-start | bytes 786440 | tf_op jit(solution)/shard_map/ppermute | solution.py:18
  343.4 675.3 %copy-start.22 = (bf16[1024,128]{1,0:T(8,128)(2,1)S(1)}, bf16[1024,128]{1,0:T(8,128)(2,1)}, u32[]{:S(2)}) copy-start(bf16[1024,128]{1,0:T(8,128)(2,1)} %get-tuple-element.2003) | copy-start | bytes 786436
  343.4 675.3 %copy-start.23 = (bf16[1024,128]{1,0:T(8,128)(2,1)S(1)}, bf16[1024,128]{1,0:T(8,128)(2,1)}, u32[]{:S(2)}) copy-start(bf16[1024,128]{1,0:T(8,128)(2,1)} %get-tuple-element.2002) | copy-start | bytes 786436
  343.4 675.3 %copy-start.24 = (bf16[1024,128]{1,0:T(8,128)(2,1)S(1)}, bf16[1024,128]{1,0:T(8,128)(2,1)}, u32[]{:S(2)}) copy-start(bf16[1024,128]{1,0:T(8,128)(2,1)} %get-tuple-element.2001) | copy-start | bytes 786436
  344.1 674.6 %copy-start.21 = (bf16[1024,128]{1,0:T(8,128)(2,1)S(1)}, bf16[1024,128]{1,0:T(8,128)(2,1)}, u32[]{:S(2)}) copy-start(bf16[1024,128]{1,0:T(8,128)(2,1)} %get-tuple-element.2004) | copy-start | bytes 786436
  344.1 675.7 %collective-permute-start.3 = (bf16[1024,128]{1,0:T(8,128)(2,1)}, bf16[1024,128]{1,0:T(8,128)(2,1)}, u32[]{:S(2)}, u32[]{:S(2)}) collective-permute-start(bf16[1024,128]{1,0:T(8,128)(2,1)} %convert_element_type.561), channel_id=1, source_target_pairs={{64,0},{128,64},{192,128},{65,1},{129,65},{193,129},{66,2},{130,66... | collective-permute-start | bytes 786440 | tf_op jit(solution)/shard_map/ppermute | solution.py:12
  (199 other events, 228.8 us)
Sparse Core Ops, SparseCore 0:
  331.8 686.8 all-reduce.4
  1021.6 42.9 all-reduce.6
